TPU v7x, 32 devices: a whole 2x2x4 slice. The times are simulated.
32 devices in a mesh: blk: 16 (over z, y, core), user: 2 (over x).
Axes of the slice: x: 2, y: 2, z: 4, core: 2. Of those that a mesh axis runs over, the one named last changes fastest.
Arguments:
- user_factors: float32 [16384, 128], P(('blk', 'user')), may hold values from -1.8 to 1.8
- item_factors: float32 [4096, 128], P(('blk', 'user')), may hold values from -1.8 to 1.8
- ratings: bfloat16 [3, 16384, 256], P(None, ('blk', 'user')), may hold values from -4 to 4
- tile_pattern: int32 [3, 128, 2], P(None, ('blk', 'user')), may hold values 0 or 1
- tile_scale: float32 [3, 128, 2], P(None, ('blk', 'user')), may hold values from 0.35 to 4.5
Outputs:
- users_out: float32 [16384, 128], P(('blk', 'user'))
- items_out: float32 [4096, 128], P(('blk', 'user'))
All inputs are finite; a program needn't handle non-finite values. No bound on the sum of `tile_pattern` on one device may be relied on, other than what follows from the above.
Results may differ from a plain program's by a relative error of at most 0.0023.
Values may be sent and summed in bfloat16 or wider, within the bound.
A program may use at most 64 MiB of HBM per device.

v0:
```python
import jax
import jax.numpy as jnp
from jax import lax
from jax.sharding import PartitionSpec as P

SUB = 3


penalty = 0.05
user_step = 0.01
item_step = 0.05
epsilon = 1e-06


def passed_along(value, axis, steps):
    count = lax.axis_size(axis)
    pairs = [(source, (source + steps) % count) for source in range(count)]
    return lax.ppermute(value, axis, pairs)


def local_pass(users, items_low, rating, pattern, scale, tile):
    rows = rating.shape[0]
    cols = rating.shape[1]
    target = (
        rating.astype(jnp.float32).reshape(rows // tile, tile, cols // tile, tile)
        * scale[:, None, :, None]
    )
    weight = pattern.astype(jnp.float32)[:, None, :, None]

    def errors(factors):
        low = factors.astype(jnp.bfloat16)
        predicted = lax.dot_general(
            low, items_low, (((1,), (1,)), ((), ())), preferred_element_type=jnp.float32
        )
        predicted = predicted.reshape(rows // tile, tile, cols // tile, tile)
        return ((weight * (predicted - target)).astype(jnp.bfloat16).reshape(rows, cols), low)

    first_err, first_low = errors(users)
    grad_users = jnp.dot(first_err, items_low, preferred_element_type=jnp.float32) + penalty * users
    users = users - user_step * grad_users
    second_err, second_low = errors(users)
    partial_value = lax.dot_general(
        second_err, second_low, (((0,), (0,)), ((), ())), preferred_element_type=jnp.float32
    )
    tile_counts = tile * jnp.sum(pattern.astype(jnp.float32), axis=0)
    counts = jnp.broadcast_to(tile_counts[:, None], (cols // tile, tile)).reshape(cols)
    return (users, partial_value, counts)


def shards(user_factors, item_factors, ratings, tile_pattern, tile_scale):
    tile = ratings.shape[2] // tile_pattern.shape[2]
    users = user_factors
    shard_rows = item_factors.shape[0]
    rank = item_factors.shape[1]
    items = item_factors
    entries = shard_rows * rank * lax.axis_size("blk") * lax.axis_size("user")
    for section in range(SUB):
        items_low = lax.all_gather(items.astype(jnp.bfloat16), "user", axis=0, tiled=True)
        users, partial_value, counts = local_pass(
            users, items_low, ratings[section], tile_pattern[section], tile_scale[section], tile
        )
        grad_share, count_share = (
            lax.psum_scatter(partial_value, "user", scatter_dimension=0, tiled=True),
            lax.psum_scatter(counts, "user", scatter_dimension=0, tiled=True),
        )
        normed = grad_share / jnp.maximum(count_share, 1.0)[:, None] + penalty * items
        squares = lax.psum(jnp.sum(normed * normed), ("blk", "user"))
        items = items - item_step * normed * lax.rsqrt(squares / entries + epsilon)
        if section < SUB - 1:
            items = passed_along(items, "blk", 1)
    return (users, items)


def solution(mesh):
    in_specs = (
        P(("blk", "user"), None),
        P(("blk", "user"), None),
        P(None, ("blk", "user"), None),
        P(None, ("blk", "user"), None),
        P(None, ("blk", "user"), None),
    )
    out_specs = (P(("blk", "user"), None), P(("blk", "user"), None))
    return jax.shard_map(shards, mesh=mesh, in_specs=in_specs, out_specs=out_specs, check_vma=False)
```

profile of v0, /device:TPU:0, one launch (start us, length us, event | category | flops | bytes accessed | tf_op | source)
XLA Modules:
  0.0 206.8 jit_solution(2798236322768383596)
XLA Ops:
  7.2 0.8 convert_bitcast_fusion
  8.0 0.1 copy.13
  8.1 0.7 slice_bitcast_fusion
  8.8 0.1 copy.14
  8.9 0.8 convert_element_type.110
  9.7 5.5 %all_gather.9 = bf16[256,128]{1,0:T(8,128)(2,1)S(1)} all-gather(bf16[128,128]{1,0:T(8,128)(2,1)S(1)} %convert_element_type.110), channel_id=1, replica_groups=mesh['blk'=16,'user'=2] {'user'}, dimensions={0}, use_global_device_ids=true | all-gather | bytes 98304 | tf_op jit(solution)/shard_map/all_gather | solution.py:58
  15.2 0.2 mul.180
  15.5 0.2 mul.183
  15.7 0.7 copy-done.3
  16.4 0.4 fusion.17
  16.8 1.2 fusion.18
  18.1 0.6 copy-done.7
  18.7 0.1 convert_reduce_fusion
  18.8 0.1 broadcast_bitcast_fusion
  19.0 0.7 copy-done.8
  19.6 0.6 dynamic-slice
  20.9 4.9 %all-reduce.3 = (f32[256]{0:T(256)S(1)}, f32[256]{0:T(256)S(1)}, f32[256]{0:T(256)S(1)}) all-reduce(f32[256]{0:T(256)S(1)} %broadcast_bitcast_fusion.2, f32[256]{0:T(256)S(1)} %broadcast_bitcast_fusion.1, f32[256]{0:T(256)S(1)} %broadcast_bitcast_fusion), channel_id=3, replica_groups=mesh['blk'=16,'user'=2] {'user'}, use_global_device_ids=true, to_apply=%region_2.0.clone | all-reduce | flops 768 | bytes 6144
  25.9 0.1 dynamic-slice_maximum_fusion.2
  25.9 4.4 %reduce-scatter.4.cloned.1.call-done = f32[128,128]{1,0:T(8,128)} async-done(((f32[256,128]{1,0:T(8,128)}), f32[128,128]{1,0:T(8,128)}) %reduce-scatter.4.cloned.1.call-update) | async-done | bytes 65552 | tf_op jit(solution)/shard_map/reduce_scatter | solution.py:63
  30.4 1.6 multiply_reduce_fusion.2
  32.0 39.5 %psum.21 = f32[]{:T(128)} all-reduce(f32[]{:T(128)} %multiply_reduce_fusion.2), channel_id=1, replica_groups=mesh['blk'=16,'user'=2] {'blk','user'}, use_global_device_ids=true, to_apply=%region_4.0 | all-reduce | flops 1 | bytes 8 | tf_op jit(solution)/shard_map/psum | solution.py:67
  72.2 0.1 multiply_subtract_fusion.2
  72.3 0.1 copy.15
  72.4 0.1 copy.16
  72.5 6.2 %collective-permute-done = f32[128,128]{1,0:T(8,128)S(1)} collective-permute-done((f32[128,128]{1,0:T(8,128)S(1)}, f32[128,128]{1,0:T(8,128)S(1)}, u32[]{:S(2)}, u32[]{:S(2)}) %collective-permute-start) | collective-permute-done | bytes 65568 | tf_op jit(solution)/shard_map/ppermute | solution.py:18
  78.7 4.8 %all_gather.10 = bf16[256,128]{1,0:T(8,128)(2,1)S(1)} all-gather(bf16[128,128]{1,0:T(8,128)(2,1)S(1)} %convert_element_type.118), channel_id=1, replica_groups=mesh['blk'=16,'user'=2] {'user'}, dimensions={0}, use_global_device_ids=true | all-gather | bytes 98304 | tf_op jit(solution)/shard_map/all_gather | solution.py:58
  83.5 0.2 mul.189
  83.7 0.2 mul.199
  83.9 0.4 fusion.15
  84.3 1.2 fusion.19
  85.6 0.1 dynamic-slice_maximum_fusion.1
  85.7 8.4 %reduce-scatter.6.cloned.1.call-done = f32[128,128]{1,0:T(8,128)} async-done(((f32[256,128]{1,0:T(8,128)}), f32[128,128]{1,0:T(8,128)}) %reduce-scatter.6.cloned.1.call-update) | async-done | bytes 65552 | tf_op jit(solution)/shard_map/reduce_scatter | solution.py:63
  94.1 1.6 multiply_reduce_fusion.1
  95.7 39.5 %psum.22 = f32[]{:T(128)} all-reduce(f32[]{:T(128)} %multiply_reduce_fusion.1), channel_id=1, replica_groups=mesh['blk'=16,'user'=2] {'blk','user'}, use_global_device_ids=true, to_apply=%region_9.0 | all-reduce | flops 1 | bytes 8 | tf_op jit(solution)/shard_map/psum | solution.py:67
  135.9 0.1 multiply_subtract_fusion.1
  136.1 0.1 copy.17
  136.2 0.1 copy.18
  136.3 6.2 %collective-permute-done.1 = f32[128,128]{1,0:T(8,128)S(1)} collective-permute-done((f32[128,128]{1,0:T(8,128)S(1)}, f32[128,128]{1,0:T(8,128)S(1)}, u32[]{:S(2)}, u32[]{:S(2)}) %collective-permute-start.1) | collective-permute-done | bytes 65568 | tf_op jit(solution)/shard_map/ppermute | solution.py:18
  142.4 4.8 %all_gather.11 = bf16[256,128]{1,0:T(8,128)(2,1)S(1)} all-gather(bf16[128,128]{1,0:T(8,128)(2,1)S(1)} %convert_element_type.126), channel_id=1, replica_groups=mesh['blk'=16,'user'=2] {'user'}, dimensions={0}, use_global_device_ids=true | all-gather | bytes 98304 | tf_op jit(solution)/shard_map/all_gather | solution.py:58
  147.3 0.2 mul.205
  147.5 0.2 mul.215
  147.7 0.4 fusion.13
  148.1 1.1 fusion.20
  149.3 0.1 dynamic-slice_maximum_fusion
  149.3 8.4 %reduce-scatter.8.cloned.1.call-done = f32[128,128]{1,0:T(8,128)} async-done(((f32[256,128]{1,0:T(8,128)}), f32[128,128]{1,0:T(8,128)}) %reduce-scatter.8.cloned.1.call-update) | async-done | bytes 65552 | tf_op jit(solution)/shard_map/reduce_scatter | solution.py:63
  157.8 1.6 multiply_reduce_fusion
  159.4 39.5 %psum.23 = f32[]{:T(128)} all-reduce(f32[]{:T(128)} %multiply_reduce_fusion), channel_id=1, replica_groups=mesh['blk'=16,'user'=2] {'blk','user'}, use_global_device_ids=true, to_apply=%region_14.0 | all-reduce | flops 1 | bytes 8 | tf_op jit(solution)/shard_map/psum | solution.py:67
  199.6 0.7 multiply_subtract_fusion
  (29 shorter events, 0.5 us)
Async XLA Ops:
  7.2 8.5 %copy-start = (bf16[3,512,256]{2,1,0:T(8,128)(2,1)S(1)}, bf16[3,512,256]{2,1,0:T(8,128)(2,1)}, u32[]{:S(2)}) copy-start(bf16[3,512,256]{2,1,0:T(8,128)(2,1)} %param.7) | copy-start | bytes 2359300
  7.2 23.2 %reduce-scatter.4.cloned.1.call-start = ((), (), s32[]{:S(2)}) async-start(), calls=%async_computation.3 | async-start | bytes 196608 | tf_op jit(solution)/shard_map/reduce_scatter | solution.py:63
  15.5 1.0 copy-start.3
  18.0 0.7 copy-start.7
  18.0 12.4 %copy-start.2 = (f32[128,128]{1,0:T(8,128)S(1)}, f32[128,128]{1,0:T(8,128)}, u32[]{:S(2)}) copy-start(f32[128,128]{1,0:T(8,128)} %param.6) | copy-start | bytes 196612
  18.0 76.1 %reduce-scatter.6.cloned.1.call-start = ((), (), s32[]{:S(2)}) async-start(), calls=%async_computation.4 | async-start | bytes 196608 | tf_op jit(solution)/shard_map/reduce_scatter | solution.py:63
  19.0 0.7 copy-start.8
  30.4 41.8 %copy-start.4 = (f32[128,128]{1,0:T(8,128)S(1)}, f32[128,128]{1,0:T(8,128)}, u32[]{:S(2)}) copy-start(f32[128,128]{1,0:T(8,128)} %reduce-scatter.4.cloned.1.call-done) | copy-start | bytes 196612
  72.3 6.4 %collective-permute-start = (f32[128,128]{1,0:T(8,128)S(1)}, f32[128,128]{1,0:T(8,128)S(1)}, u32[]{:S(2)}, u32[]{:S(2)}) collective-permute-start(f32[128,128]{1,0:T(8,128)S(1)} %multiply_subtract_fusion.2), channel_id=1, source_target_pairs={{0,2},{2,4},{4,6},{6,8},{8,10},{10,12},{12,14},{14,16},{16,18},{18... | collective-permute-start | bytes 196616 | tf_op jit(solution)/shard_map/ppermute | solution.py:18
  85.5 72.2 %reduce-scatter.8.cloned.1.call-start = ((), (), s32[]{:S(2)}) async-start(), calls=%async_computation.5 | async-start | bytes 196608 | tf_op jit(solution)/shard_map/reduce_scatter | solution.py:63
  94.1 41.8 %copy-start.6 = (f32[128,128]{1,0:T(8,128)S(1)}, f32[128,128]{1,0:T(8,128)}, u32[]{:S(2)}) copy-start(f32[128,128]{1,0:T(8,128)} %reduce-scatter.6.cloned.1.call-done) | copy-start | bytes 196612
  136.0 6.4 %collective-permute-start.1 = (f32[128,128]{1,0:T(8,128)S(1)}, f32[128,128]{1,0:T(8,128)S(1)}, u32[]{:S(2)}, u32[]{:S(2)}) collective-permute-start(f32[128,128]{1,0:T(8,128)S(1)} %multiply_subtract_fusion.1), channel_id=1, source_target_pairs={{0,2},{2,4},{4,6},{6,8},{8,10},{10,12},{12,14},{14,16},{16,18},{18... | collective-permute-start | bytes 196616 | tf_op jit(solution)/shard_map/ppermute | solution.py:18
  148.1 1.2 copy-start.1
  157.8 41.8 %copy-start.5 = (f32[128,128]{1,0:T(8,128)S(1)}, f32[128,128]{1,0:T(8,128)}, u32[]{:S(2)}) copy-start(f32[128,128]{1,0:T(8,128)} %reduce-scatter.8.cloned.1.call-done) | copy-start | bytes 196612
Sparse Core Ops, SparseCore 0:
  18.1 12.2 reduce-scatter.3
  85.6 8.3 reduce-scatter.5
  149.4 8.3 reduce-scatter.7
where the time goes:
time: 208 us; the launch traced here: 207 us
  blocking collectives  138 us (66%)
  waiting for transfers between devices  33.7 us (16%)
  between operations  16.6 us (8%)
  other arithmetic  7.75 us (4%)
  local copies, waits for them, and re-layouts  5.29 us (3%)
  matrix products  4.7 us (2%)
    psum x3, blocking collectives, shards(): squares = lax.psum(jnp.sum(normed * normed), ('blk', 'user'))  118 us
    reduce_scatter x3, waiting for transfers between devices, shards(): lax.psum_scatter(partial_value, 'user', scatter_dimension=0, tiled=True)  21.3 us
    all_gather x3, blocking collectives, shards(): lax.all_gather(items.astype(jnp.bfloat16), 'user', axis=0, tiled=True)  15.1 us
    ppermute x2, waiting for transfers between devices, passed_along(): return lax.ppermute(value, axis, pairs)  12.4 us
    unnamed x1, blocking collectives  4.92 us
    reduce_sum x3, other arithmetic, shards(): squares = lax.psum(jnp.sum(normed * normed), ('blk', 'user'))  4.82 us
  transfers between devices with their start and end apart: 5, of which 5 were waited for; matrix products, arithmetic and copies ran while one was open for 1% of the time, Pallas kernels for 0%

commit v1 on v0

v1 whole, which is shorter than its diff:
```python
import functools

import jax
import jax.numpy as jnp
from jax import lax
from jax.experimental import pallas as pl
from jax.experimental.pallas import tpu as pltpu
from jax.sharding import PartitionSpec as P

SUB = 3

penalty = 0.05
user_step = 0.01
item_step = 0.05
epsilon = 1e-06

MESH = pl.DeviceIdType.MESH
F32 = jnp.float32
BF16 = jnp.bfloat16
NT = (((1,), (1,)), ((), ()))
TN = (((0,), (0,)), ((), ()))


def wait_bytes(ref, sem):
    pltpu.make_async_copy(ref, ref, sem).wait()


def kernel(nb, nu, tile, u_hbm, v_hbm, r_hbm, pat, scl, uo_hbm, vo_hbm,
           u, rating, target, vlow, vfull, v_f32, ulow, err, cnt, cnt_in,
           psend, precv, part, nsend, nrecv, ss, ss_in, vout,
           u_sem, v_sem, r_sem, out_sem, c_send, c_recv, vl_send, vl_recv,
           vf_send, vf_recv, p_send, p_recv, fw_send, fw_recv, n_send, n_recv,
           s_send, s_recv):
    rows, rank = u.shape
    cols = rating.shape[2]
    share = v_hbm.shape[0]
    rt, ct = rows // tile, cols // tile
    g = lax.axis_index("blk")
    w = lax.axis_index("user")
    mine = pl.ds(pl.multiple_of(w * share, share), share)
    nxt = {"blk": lax.rem(g + 1, nb)}

    load_v = pltpu.make_async_copy(v_hbm, vfull.at[0, mine], v_sem)
    load_u = pltpu.make_async_copy(u_hbm, u, u_sem)
    loads = [pltpu.make_async_copy(r_hbm.at[s], rating.at[s], r_sem.at[s]) for s in range(SUB)]
    load_v.start()
    load_u.start()
    for copy in loads:
        copy.start()

    barrier = pltpu.get_barrier_semaphore()
    for d in range(1, nb):
        pl.semaphore_signal(barrier, inc=1, device_id={"blk": lax.rem(g + d, nb)}, device_id_type=MESH)
    for d in range(1, nu):
        pl.semaphore_signal(barrier, inc=1, device_id={"user": lax.rem(w + d, nu)}, device_id_type=MESH)

    for s in range(SUB):
        for j in range(ct):
            total = pat[s, 0, j]
            for a in range(1, rt):
                total = total + pat[s, a, j]
            cnt[pl.ds(s * ct + j, 1), :] = jnp.full((1, rank), (total * tile).astype(F32))
    load_v.wait()
    vlow[mine, :] = vfull[0, mine, :].astype(BF16)

    def make_target(s):
        loads[s].wait()
        for a in range(rt):
            for j in range(ct):
                block = (slice(a * tile, (a + 1) * tile), slice(j * tile, (j + 1) * tile))
                target[(s,) + block] = rating[(s,) + block].astype(F32) * scl[s, a, j]

    pl.semaphore_wait(barrier, nb - 1 + nu - 1)

    sends = []

    def send(src, dst, one, two, where):
        copy = pltpu.make_async_remote_copy(
            src_ref=src, dst_ref=dst, send_sem=one, recv_sem=two, device_id=where, device_id_type=MESH
        )
        copy.start()
        return copy

    others = [{"user": lax.rem(w + d, nu)} for d in range(1, nu)]
    first = []
    for d, where in enumerate(others):
        first.append(send(vlow.at[mine], vlow.at[mine], vl_send.at[d], vl_recv.at[d], where))
    for d, where in enumerate(others):
        first.append(send(vfull.at[0, mine], vfull.at[0, mine], vf_send.at[d], vf_recv.at[d], where))
        first.append(send(cnt, cnt_in.at[d], c_send.at[d], c_recv.at[d], where))

    make_target(0)
    load_u.wait()

    for s in range(SUB):
        last = s == SUB - 1
        if s == 0:
            for copy in first[: nu - 1]:
                copy.wait_recv()
        v_low = vlow[...]

        def errors(low, a):
            predicted = lax.dot_general(low, v_low, NT, preferred_element_type=F32)
            out = []
            for j in range(ct):
                columns = slice(j * tile, (j + 1) * tile)
                diff = predicted[:, columns] - target[s, a * tile:(a + 1) * tile, columns]
                out.append((pat[s, a, j].astype(F32) * diff).astype(BF16))
            return jnp.concatenate(out, axis=1)

        for a in range(rt):
            span = slice(a * tile, (a + 1) * tile)
            old = u[span, :]
            one = errors(old.astype(BF16), a)
            grad = jnp.dot(one, v_low, preferred_element_type=F32) + penalty * old
            new = old - user_step * grad
            u[span, :] = new
            low = new.astype(BF16)
            ulow[span, :] = low
            err[span, :] = errors(low, a)

        exchanged = []
        for j in range(ct):
            columns = slice(j * tile, (j + 1) * tile)
            value = lax.dot_general(err[:, columns], ulow[...], TN, preferred_element_type=F32)
            part[columns, :] = value
            psend[s, columns, :] = value.astype(BF16)
            for d, where in enumerate(others):
                exchanged.append(send(
                    psend.at[s, columns], precv.at[s, d, columns], p_send.at[s, d, j], p_recv.at[s, d, j], where
                ))

        if last:
            store_u = pltpu.make_async_copy(u, uo_hbm, u_sem)
            store_u.start()
        if s == 0:
            for copy in first[nu - 1:]:
                copy.wait_recv()
            for copy in first:
                copy.wait_send()
            total = cnt[...]
            for d in range(nu - 1):
                total = total + cnt_in[d]
            cnt[...] = 1.0 / jnp.maximum(total, 1.0)
        if not last:
            forward = send(vfull.at[s], vfull.at[s + 1], fw_send.at[s], fw_recv.at[s], nxt)
            make_target(s + 1)

        squares = jnp.zeros((8, rank), F32)
        for j in range(ct):
            columns = slice(j * tile, (j + 1) * tile)
            for d in range(nu - 1):
                exchanged[j * (nu - 1) + d].wait()
            total = part[columns, :]
            for d in range(nu - 1):
                total = total + precv[s, d, columns, :].astype(F32)
            v_old = vfull[s, columns, :] if s == 0 else v_f32[columns, :]
            normed = total * cnt[pl.ds(s * ct + j, 1), :] + penalty * v_old
            squares = squares + jnp.sum((normed * normed).reshape(tile // 8, 8, rank), axis=0)
            if last:
                part[columns, :] = normed
            else:
                nsend[s, columns, :] = normed.astype(BF16)
        ss[s] = jnp.sum(squares, axis=0, keepdims=True)
        for d in range(1, nb):
            send(ss.at[s], ss_in.at[s, d - 1], s_send.at[s], s_recv.at[s], {"blk": lax.rem(g + d, nb)})
        if not last:
            ahead = send(nsend.at[s], nrecv.at[s], n_send.at[s], n_recv.at[s], nxt)

        wait_bytes(ss_in.at[s], s_recv.at[s])
        total = ss[s] + jnp.sum(ss_in[s], axis=0)
        mean = jnp.sum(total, axis=1, keepdims=True) / (nb * cols * rank)
        gain = item_step * lax.rsqrt(mean + epsilon)
        if not last:
            forward.wait()
            ahead.wait()
            fresh = vfull[s + 1] - gain * nrecv[s].astype(F32)
            v_f32[...] = fresh
            vlow[...] = fresh.astype(BF16)
            if s + 1 < SUB - 1:
                vfull[s + 1] = fresh
        else:
            vout[...] = v_f32[mine, :] - gain * part[mine, :]
            store_v = pltpu.make_async_copy(vout, vo_hbm, v_sem)
            store_v.start()
    for s in range(SUB):
        wait_bytes(ss_in.at[s], s_send.at[s])
    store_u.wait()
    store_v.wait()


def shards(user_factors, item_factors, ratings, tile_pattern, tile_scale):
    nb, nu = lax.axis_size("blk"), lax.axis_size("user")
    tile = ratings.shape[2] // tile_pattern.shape[2]
    rows, rank = user_factors.shape
    share = item_factors.shape[0]
    cols = ratings.shape[2]
    ct = cols // tile
    counts = -(-SUB * ct // 8) * 8
    dma = pltpu.SemaphoreType.DMA
    vmem = pltpu.VMEM
    hbm = pl.BlockSpec(memory_space=pl.ANY)
    smem = pl.BlockSpec(memory_space=pltpu.SMEM)
    return pl.pallas_call(
        functools.partial(kernel, nb, nu, tile),
        out_shape=(
            jax.ShapeDtypeStruct(user_factors.shape, F32),
            jax.ShapeDtypeStruct(item_factors.shape, F32),
        ),
        in_specs=[hbm, hbm, hbm, smem, smem],
        out_specs=(hbm, hbm),
        scratch_shapes=[
            vmem((rows, rank), F32),
            vmem((SUB, rows, cols), BF16),
            vmem((SUB, rows, cols), F32),
            vmem((cols, rank), BF16),
            vmem((SUB, cols, rank), F32),
            vmem((cols, rank), F32),
            vmem((rows, rank), BF16),
            vmem((rows, cols), BF16),
            vmem((counts, rank), F32),
            vmem((nu - 1, counts, rank), F32),
            vmem((SUB, cols, rank), BF16),
            vmem((SUB, nu - 1, cols, rank), BF16),
            vmem((cols, rank), F32),
            vmem((SUB - 1, cols, rank), BF16),
            vmem((SUB - 1, cols, rank), BF16),
            vmem((SUB, 1, rank), F32),
            vmem((SUB, nb - 1, 1, rank), F32),
            vmem((share, rank), F32),
            dma(()), dma(()), dma((SUB,)), dma(()),
            dma((nu - 1,)), dma((nu - 1,)),
            dma((nu - 1,)), dma((nu - 1,)),
            dma((nu - 1,)), dma((nu - 1,)),
            dma((SUB, nu - 1, ct)), dma((SUB, nu - 1, ct)),
            dma((SUB - 1,)), dma((SUB - 1,)),
            dma((SUB - 1,)), dma((SUB - 1,)),
            dma((SUB,)), dma((SUB,)),
        ],
        compiler_params=pltpu.CompilerParams(collective_id=0, has_side_effects=True),
    )(user_factors, item_factors, ratings, tile_pattern, tile_scale)


def solution(mesh):
    specs = (
        P(("blk", "user"), None),
        P(("blk", "user"), None),
        P(None, ("blk", "user"), None),
        P(None, ("blk", "user"), None),
        P(None, ("blk", "user"), None),
    )
    out_specs = (P(("blk", "user"), None), P(("blk", "user"), None))
    return jax.shard_map(shards, mesh=mesh, in_specs=specs, out_specs=out_specs, check_vma=False)
```

time: 208 us -> 40.8 us (0.20)
  blocking collectives: 138 us -> 0 us
  Pallas kernels: 0 us -> 35.5 us
  waiting for transfers between devices: 33.7 us -> 0 us
  between operations: 16.6 us -> 0.66 us
  other arithmetic: 7.75 us -> 0 us
  matrix products: 4.7 us -> 0 us
    psum x3 -> x0, blocking collectives: 118 us -> none  [shards(): squares = lax.psum(jnp.sum(normed * normed), ('blk', 'user'))]
    pallas_call x0 -> x1, Pallas kernels: none -> 35.5 us  [shards(): pl.pallas_call(functools.partial(kernel, nb, nu, tile), out_shape=(jax.Sh...]
    reduce_scatter x3 -> x0, waiting for transfers between devices: 21.3 us -> none  [shards(): lax.psum_scatter(partial_value, 'user', scatter_dimension=0, tiled=True)]
    all_gather x3 -> x0, blocking collectives: 15.1 us -> none  [shards(): lax.all_gather(items.astype(jnp.bfloat16), 'user', axis=0, tiled=True)]
    ppermute x2 -> x0, waiting for transfers between devices: 12.4 us -> none  [passed_along(): return lax.ppermute(value, axis, pairs)]
    reduce_sum x4 -> x0, other arithmetic: 4.97 us -> none  [the longest x3 4.82 us: shards(): squares = lax.psum(jnp.sum(normed * normed), ('blk', 'user'))]
    unnamed x1 -> x0, blocking collectives: 4.92 us -> none
    dot_general x6 -> x0, matrix products: 4.7 us -> none  [the longest x3 3.48 us: local_pass(): lax.dot_general(second_err, second_low, (((0,), (0,)), ((), ())), preferr...]
  transfers between devices with their start and end apart: 5 -> 0, of which waited for: 5 -> 0; matrix products, arithmetic and copies ran while one was open for 1% -> 0% of each run, Pallas kernels for 0% -> 0%
where the time goes in v1:
time: 40.8 us; the launch traced here: 40.5 us
  Pallas kernels  35.5 us (87%)
  local copies, waits for them, and re-layouts  4.4 us (11%)
  between operations  0.66 us (2%)
    pallas_call x1, Pallas kernels, shards(): pl.pallas_call(functools.partial(kernel, nb, nu, tile), out_shape=(jax.Sh...  35.5 us
    unnamed x8, local copies, waits for them, and re-layouts  4.4 us

profile of v1, /device:TPU:0, one launch (start us, length us, event | category | flops | bytes accessed | tf_op | source)
XLA Modules:
  0.0 40.5 jit_solution(13919890643523663104)
XLA Ops:
  0.6 0.0 copy-start.1
  0.6 1.4 %copy.7.pat = s32[3,4,2]{2,1,0:T(4,128)} copy(s32[3,4,2]{1,2,0:T(2,128)} %param.8) | data formatting | bytes 192 | tf_op args[3]
  2.0 0.0 copy-done.1
  2.0 0.7 %copy.8.scl = f32[3,4,2]{2,1,0:T(4,128)} copy(f32[3,4,2]{1,2,0:T(2,128)S(1)} %copy-done.1) | data formatting | bytes 192 | tf_op args[4]
  2.7 35.5 %shard_map.68 = (f32[512,128]{1,0:T(8,128)}, f32[128,128]{1,0:T(8,128)}) custom-call(f32[512,128]{1,0:T(8,128)} %u_hbm.1, f32[128,128]{1,0:T(8,128)} %v_hbm.1, bf16[3,512,256]{2,1,0:T(8,128)(2,1)} %r_hbm.1, s32[3,4,2]{2,1,0:T(4,128)} %copy.7.pat, f32[3,4,2]{2,1,0:T(4,128)} %copy.8.scl), custom_call_target="tpu_custom_call" | custom-call | tf_op jit(solution)/shard_map/pallas_call | solution.py:204
  38.2 0.0 copy-start
  38.2 1.7 %copy.11 = f32[512,128]{1,0:T(8,128)} copy(f32[512,128]{1,0:T(8,128)} %get-tuple-element.4) | data formatting | bytes 524288
  39.9 0.0 copy-done
  39.9 0.6 %copy.12 = f32[128,128]{1,0:T(8,128)} copy(f32[128,128]{1,0:T(8,128)S(1)} %copy-done) | data formatting | bytes 131072
Async XLA Ops:
  0.6 1.4 %copy-start.1 = (f32[3,4,2]{1,2,0:T(2,128)S(1)}, f32[3,4,2]{1,2,0:T(2,128)}, u32[]{:S(2)}) copy-start(f32[3,4,2]{1,2,0:T(2,128)} %param.9) | copy-start | bytes 292
  38.2 1.7 %copy-start = (f32[128,128]{1,0:T(8,128)S(1)}, f32[128,128]{1,0:T(8,128)}, u32[]{:S(2)}) copy-start(f32[128,128]{1,0:T(8,128)} %get-tuple-element.5) | copy-start | bytes 196612

commit v2 on v1

--- a/solution.py
+++ b/solution.py
@@ -8,6 +8,8 @@
 from jax.sharding import PartitionSpec as P
 
 SUB = 3
+SIDES = (1, 2)
+LAYER = 4
 
 penalty = 0.05
 user_step = 0.01
@@ -25,12 +27,12 @@
     pltpu.make_async_copy(ref, ref, sem).wait()
 
 
-def kernel(nb, nu, tile, u_hbm, v_hbm, r_hbm, pat, scl, uo_hbm, vo_hbm,
-           u, rating, target, vlow, vfull, v_f32, ulow, err, cnt, cnt_in,
-           psend, precv, part, nsend, nrecv, ss, ss_in, vout,
-           u_sem, v_sem, r_sem, out_sem, c_send, c_recv, vl_send, vl_recv,
+def kernel(nb, nu, tile, u_hbm, v_hbm, r_hbm, pat, scl, u, vout,
+           rating, target, vlow, vfull, v_f32, ulow, err, cnt, cnt_in,
+           psend, precv, part, nsend, nrecv, ss, ss_in,
+           u_sem, v_sem, r_sem, c_send, c_recv, vl_send, vl_recv,
            vf_send, vf_recv, p_send, p_recv, fw_send, fw_recv, n_send, n_recv,
-           s_send, s_recv):
+           s_send, s_recv, up_sem, down_sem, side_sem):
     rows, rank = u.shape
     cols = rating.shape[2]
     share = v_hbm.shape[0]
@@ -49,16 +51,36 @@
         copy.start()
 
     barrier = pltpu.get_barrier_semaphore()
-    for d in range(1, nb):
-        pl.semaphore_signal(barrier, inc=1, device_id={"blk": lax.rem(g + d, nb)}, device_id_type=MESH)
+    def signal(sem, where):
+        pl.semaphore_signal(sem, inc=1, device_id=where, device_id_type=MESH)
+
+    layers = nb // LAYER
+    z = lax.div(g, LAYER)
+    below, above = z > 0, z < layers - 1
+    lower = {"blk": lax.rem(g + nb - LAYER, nb)}
+    upper = {"blk": lax.rem(g + LAYER, nb)}
+    beside = [{"blk": g + d - 2 * d * lax.rem(lax.div(g, d), 2)} for d in SIDES]
     for d in range(1, nu):
-        pl.semaphore_signal(barrier, inc=1, device_id={"user": lax.rem(w + d, nu)}, device_id_type=MESH)
+        signal(barrier, {"user": lax.rem(w + d, nu)})
+    for where in beside:
+        signal(barrier, where)
+    pl.when(below)(lambda: signal(barrier, lower))
+    pl.when(above)(lambda: signal(barrier, upper))
+    greeted = nu - 1 + len(SIDES) + below.astype(jnp.int32) + above.astype(jnp.int32)
+
+    def upward():
+        pl.when(below)(lambda: pl.semaphore_wait(up_sem, 1))
+        pl.when(above)(lambda: signal(up_sem, upper))
+
+    def downward():
+        pl.when(above)(lambda: pl.semaphore_wait(down_sem, 1))
+        pl.when(below)(lambda: signal(down_sem, lower))
 
     for s in range(SUB):
         for j in range(ct):
-            total = pat[s, 0, j]
+            total = pat[s, j, 0]
             for a in range(1, rt):
-                total = total + pat[s, a, j]
+                total = total + pat[s, j, a]
             cnt[pl.ds(s * ct + j, 1), :] = jnp.full((1, rank), (total * tile).astype(F32))
     load_v.wait()
     vlow[mine, :] = vfull[0, mine, :].astype(BF16)
@@ -68,9 +90,9 @@
         for a in range(rt):
             for j in range(ct):
                 block = (slice(a * tile, (a + 1) * tile), slice(j * tile, (j + 1) * tile))
-                target[(s,) + block] = rating[(s,) + block].astype(F32) * scl[s, a, j]
-
-    pl.semaphore_wait(barrier, nb - 1 + nu - 1)
+                target[(s,) + block] = rating[(s,) + block].astype(F32) * scl[s, j, a]
+
+    pl.semaphore_wait(barrier, greeted)
 
     sends = []
 
@@ -89,6 +111,17 @@
         first.append(send(vfull.at[0, mine], vfull.at[0, mine], vf_send.at[d], vf_recv.at[d], where))
         first.append(send(cnt, cnt_in.at[d], c_send.at[d], c_recv.at[d], where))
 
+    @pl.when(2 * z < layers)
+    def _():
+        upward()
+        downward()
+
+    @pl.when(2 * z >= layers)
+    def _():
+        downward()
+        upward()
+
+    signal(side_sem.at[0], beside[0])
     make_target(0)
     load_u.wait()
 
@@ -97,6 +130,9 @@
         if s == 0:
             for copy in first[: nu - 1]:
                 copy.wait_recv()
+            for k in range(1, len(SIDES)):
+                pl.semaphore_wait(side_sem.at[k - 1], 1)
+                signal(side_sem.at[k], beside[k])
         v_low = vlow[...]
 
         def errors(low, a):
@@ -105,7 +141,7 @@
             for j in range(ct):
                 columns = slice(j * tile, (j + 1) * tile)
                 diff = predicted[:, columns] - target[s, a * tile:(a + 1) * tile, columns]
-                out.append((pat[s, a, j].astype(F32) * diff).astype(BF16))
+                out.append((pat[s, j, a].astype(F32) * diff).astype(BF16))
             return jnp.concatenate(out, axis=1)
 
         for a in range(rt):
@@ -130,10 +166,8 @@
                     psend.at[s, columns], precv.at[s, d, columns], p_send.at[s, d, j], p_recv.at[s, d, j], where
                 ))
 
-        if last:
-            store_u = pltpu.make_async_copy(u, uo_hbm, u_sem)
-            store_u.start()
         if s == 0:
+            pl.semaphore_wait(side_sem.at[len(SIDES) - 1], 1)
             for copy in first[nu - 1:]:
                 copy.wait_recv()
             for copy in first:
@@ -160,7 +194,7 @@
             if last:
                 part[columns, :] = normed
             else:
-                nsend[s, columns, :] = normed.astype(BF16)
+                nsend[s, columns, :] = normed
         ss[s] = jnp.sum(squares, axis=0, keepdims=True)
         for d in range(1, nb):
             send(ss.at[s], ss_in.at[s, d - 1], s_send.at[s], s_recv.at[s], {"blk": lax.rem(g + d, nb)})
@@ -181,12 +215,16 @@
                 vfull[s + 1] = fresh
         else:
             vout[...] = v_f32[mine, :] - gain * part[mine, :]
-            store_v = pltpu.make_async_copy(vout, vo_hbm, v_sem)
-            store_v.start()
     for s in range(SUB):
         wait_bytes(ss_in.at[s], s_send.at[s])
-    store_u.wait()
-    store_v.wait()
+
+
+def hand_over(u, v, uo_hbm, vo_hbm, sem):
+    copies = [pltpu.make_async_copy(v, vo_hbm, sem.at[0]), pltpu.make_async_copy(u, uo_hbm, sem.at[1])]
+    for copy in copies:
+        copy.start()
+    for copy in copies:
+        copy.wait()
 
 
 def shards(user_factors, item_factors, ratings, tile_pattern, tile_scale):
@@ -200,17 +238,14 @@
     dma = pltpu.SemaphoreType.DMA
     vmem = pltpu.VMEM
     hbm = pl.BlockSpec(memory_space=pl.ANY)
+    whole = pl.BlockSpec(memory_space=pltpu.VMEM)
     smem = pl.BlockSpec(memory_space=pltpu.SMEM)
-    return pl.pallas_call(
+    users, items = pl.pallas_call(
         functools.partial(kernel, nb, nu, tile),
-        out_shape=(
-            jax.ShapeDtypeStruct(user_factors.shape, F32),
-            jax.ShapeDtypeStruct(item_factors.shape, F32),
-        ),
+        out_shape=(vmem(user_factors.shape, F32), vmem(item_factors.shape, F32)),
         in_specs=[hbm, hbm, hbm, smem, smem],
-        out_specs=(hbm, hbm),
+        out_specs=(whole, whole),
         scratch_shapes=[
-            vmem((rows, rank), F32),
             vmem((SUB, rows, cols), BF16),
             vmem((SUB, rows, cols), F32),
             vmem((cols, rank), BF16),
@@ -223,12 +258,11 @@
             vmem((SUB, cols, rank), BF16),
             vmem((SUB, nu - 1, cols, rank), BF16),
             vmem((cols, rank), F32),
-            vmem((SUB - 1, cols, rank), BF16),
-            vmem((SUB - 1, cols, rank), BF16),
+            vmem((SUB - 1, cols, rank), F32),
+            vmem((SUB - 1, cols, rank), F32),
             vmem((SUB, 1, rank), F32),
             vmem((SUB, nb - 1, 1, rank), F32),
-            vmem((share, rank), F32),
-            dma(()), dma(()), dma((SUB,)), dma(()),
+            dma(()), dma(()), dma((SUB,)),
             dma((nu - 1,)), dma((nu - 1,)),
             dma((nu - 1,)), dma((nu - 1,)),
             dma((nu - 1,)), dma((nu - 1,)),
@@ -236,9 +270,21 @@
             dma((SUB - 1,)), dma((SUB - 1,)),
             dma((SUB - 1,)), dma((SUB - 1,)),
             dma((SUB,)), dma((SUB,)),
+            pltpu.SemaphoreType.REGULAR, pltpu.SemaphoreType.REGULAR,
+            pltpu.SemaphoreType.REGULAR((len(SIDES),)),
         ],
         compiler_params=pltpu.CompilerParams(collective_id=0, has_side_effects=True),
-    )(user_factors, item_factors, ratings, tile_pattern, tile_scale)
+    )(user_factors, item_factors, ratings, jnp.swapaxes(tile_pattern, 1, 2), jnp.swapaxes(tile_scale, 1, 2))
+    return pl.pallas_call(
+        hand_over,
+        out_shape=(
+            jax.ShapeDtypeStruct(user_factors.shape, F32),
+            jax.ShapeDtypeStruct(item_factors.shape, F32),
+        ),
+        in_specs=[whole, whole],
+        out_specs=(hbm, hbm),
+        scratch_shapes=[dma((2,))],
+    )(pltpu.with_memory_space_constraint(users, pltpu.VMEM), pltpu.with_memory_space_constraint(items, pltpu.VMEM))
 
 
 def solution(mesh):

time: 40.8 us -> 36.2 us (0.89)
  local copies, waits for them, and re-layouts: 4.4 us -> 0 us
    unnamed x8 -> x0, local copies, waits for them, and re-layouts: 4.4 us -> none
    pallas_call x1 -> x2, Pallas kernels: 35.5 us -> 35.4 us  [the longest x1 34.7 us: shards(): pl.pallas_call(functools.partial(kernel, nb, nu, tile), out_shape=(vmem(u...]
where the time goes in v2:
time: 36.2 us; the launch traced here: 36 us
  Pallas kernels  35.4 us (98%)
  between operations  0.64 us (2%)
    pallas_call x1, Pallas kernels, shards(): pl.pallas_call(functools.partial(kernel, nb, nu, tile), out_shape=(vmem(u...  34.7 us
    pallas_call x1, Pallas kernels, shards(): pl.pallas_call(hand_over, out_shape=(jax.ShapeDtypeStruct(user_factors.sh...  0.74 us

profile of v2, /device:TPU:0, one launch (start us, length us, event | category | flops | bytes accessed | tf_op | source)
XLA Modules:
  0.0 36.0 jit_solution(983026537425566071)
XLA Ops:
  0.6 34.7 %shard_map.68 = (f32[512,128]{1,0:T(8,128)S(1)}, f32[128,128]{1,0:T(8,128)S(1)}) custom-call(f32[512,128]{1,0:T(8,128)} %u_hbm.1, f32[128,128]{1,0:T(8,128)} %v_hbm.1, bf16[3,512,256]{2,1,0:T(8,128)(2,1)} %r_hbm.1, s32[3,2,4]{2,1,0:T(2,128)} %bitcast.2, f32[3,2,4]{2,1,0:T(2,128)} %bitcast.3), custom_call_target="tpu_custom_call" | custom-call | tf_op jit(solution)/shard_map/pallas_call | solution.py:243
  35.3 0.7 %shard_map.69 = (f32[512,128]{1,0:T(8,128)}, f32[128,128]{1,0:T(8,128)}) custom-call(f32[512,128]{1,0:T(8,128)S(1)} %get-tuple-element.4.u, f32[128,128]{1,0:T(8,128)S(1)} %get-tuple-element.5.v), custom_call_target="tpu_custom_call" | custom-call | tf_op jit(solution)/shard_map/pallas_call | solution.py:278

commit v3 on v2

--- a/solution.py
+++ b/solution.py
@@ -32,7 +32,8 @@
            psend, precv, part, nsend, nrecv, ss, ss_in,
            u_sem, v_sem, r_sem, c_send, c_recv, vl_send, vl_recv,
            vf_send, vf_recv, p_send, p_recv, fw_send, fw_recv, n_send, n_recv,
-           s_send, s_recv, up_sem, down_sem, side_sem):
+           s_send, s_recv, up_sem, down_sem, side_sem,
+           rating_p, target_p, u_p, meta, meta_in, m_send, m_recv):
     rows, rank = u.shape
     cols = rating.shape[2]
     share = v_hbm.shape[0]
@@ -82,6 +83,16 @@
             for a in range(1, rt):
                 total = total + pat[s, j, a]
             cnt[pl.ds(s * ct + j, 1), :] = jnp.full((1, rank), (total * tile).astype(F32))
+    mirrored = nu == 2
+
+    def meta_row(kind, a, j):
+        return pl.ds((kind * rt + a) * ct + j, 1)
+
+    if mirrored:
+        for a in range(rt):
+            for j in range(ct):
+                meta[meta_row(0, a, j), :] = jnp.full((1, tile), pat[SUB - 1, j, a].astype(F32))
+                meta[meta_row(1, a, j), :] = jnp.full((1, tile), scl[SUB - 1, j, a])
     load_v.wait()
     vlow[mine, :] = vfull[0, mine, :].astype(BF16)
 
@@ -110,6 +121,9 @@
     for d, where in enumerate(others):
         first.append(send(vfull.at[0, mine], vfull.at[0, mine], vf_send.at[d], vf_recv.at[d], where))
         first.append(send(cnt, cnt_in.at[d], c_send.at[d], c_recv.at[d], where))
+
+    if mirrored:
+        meta_ahead = send(meta, meta_in, m_send.at[2], m_recv.at[2], others[0])
 
     @pl.when(2 * z < layers)
     def _():
@@ -135,31 +149,54 @@
                 signal(side_sem.at[k], beside[k])
         v_low = vlow[...]
 
-        def errors(low, a):
+        both = mirrored and last
+        if both:
+            users_ahead.wait()
+
+        def own_tile(a, j):
+            return (
+                pat[s, j, a].astype(F32),
+                target[s, a * tile:(a + 1) * tile, j * tile:(j + 1) * tile],
+            )
+
+        def partner_tile(a, j):
+            return (
+                meta_in[meta_row(0, a, j), :],
+                target_p[a * tile:(a + 1) * tile, j * tile:(j + 1) * tile],
+            )
+
+        def errors(low, a, tile_of):
             predicted = lax.dot_general(low, v_low, NT, preferred_element_type=F32)
             out = []
             for j in range(ct):
-                columns = slice(j * tile, (j + 1) * tile)
-                diff = predicted[:, columns] - target[s, a * tile:(a + 1) * tile, columns]
-                out.append((pat[s, j, a].astype(F32) * diff).astype(BF16))
+                weight, goal = tile_of(a, j)
+                diff = predicted[:, j * tile:(j + 1) * tile] - goal
+                out.append((weight * diff).astype(BF16))
             return jnp.concatenate(out, axis=1)
 
+        sets = [(u, 0, own_tile)] + ([(u_p, rows, partner_tile)] if both else [])
         for a in range(rt):
-            span = slice(a * tile, (a + 1) * tile)
-            old = u[span, :]
-            one = errors(old.astype(BF16), a)
-            grad = jnp.dot(one, v_low, preferred_element_type=F32) + penalty * old
-            new = old - user_step * grad
-            u[span, :] = new
-            low = new.astype(BF16)
-            ulow[span, :] = low
-            err[span, :] = errors(low, a)
+            for held, start, tile_of in sets:
+                span = slice(a * tile, (a + 1) * tile)
+                place = slice(start + a * tile, start + (a + 1) * tile)
+                old = held[span, :].astype(F32)
+                one = errors(old.astype(BF16), a, tile_of)
+                grad = jnp.dot(one, v_low, preferred_element_type=F32) + penalty * old
+                new = old - user_step * grad
+                if held is u:
+                    u[span, :] = new
+                low = new.astype(BF16)
+                ulow[place, :] = low
+                err[place, :] = errors(low, a, tile_of)
 
         exchanged = []
         for j in range(ct):
             columns = slice(j * tile, (j + 1) * tile)
-            value = lax.dot_general(err[:, columns], ulow[...], TN, preferred_element_type=F32)
+            deep = slice(0, len(sets) * rows)
+            value = lax.dot_general(err[deep, columns], ulow[deep, :], TN, preferred_element_type=F32)
             part[columns, :] = value
+            if both:
+                continue
             psend[s, columns, :] = value.astype(BF16)
             for d, where in enumerate(others):
                 exchanged.append(send(
@@ -179,14 +216,21 @@
         if not last:
             forward = send(vfull.at[s], vfull.at[s + 1], fw_send.at[s], fw_recv.at[s], nxt)
             make_target(s + 1)
+        if mirrored and s == SUB - 2:
+            ratings_ahead.wait()
+            meta_ahead.wait()
+            for a in range(rt):
+                for j in range(ct):
+                    block = (slice(a * tile, (a + 1) * tile), slice(j * tile, (j + 1) * tile))
+                    target_p[block] = rating_p[block].astype(F32) * meta_in[meta_row(1, a, j), :]
 
         squares = jnp.zeros((8, rank), F32)
         for j in range(ct):
             columns = slice(j * tile, (j + 1) * tile)
-            for d in range(nu - 1):
+            for d in range(0 if both else nu - 1):
                 exchanged[j * (nu - 1) + d].wait()
             total = part[columns, :]
-            for d in range(nu - 1):
+            for d in range(0 if both else nu - 1):
                 total = total + precv[s, d, columns, :].astype(F32)
             v_old = vfull[s, columns, :] if s == 0 else v_f32[columns, :]
             normed = total * cnt[pl.ds(s * ct + j, 1), :] + penalty * v_old
@@ -201,6 +245,10 @@
         if not last:
             ahead = send(nsend.at[s], nrecv.at[s], n_send.at[s], n_recv.at[s], nxt)
 
+        if mirrored and s == 0:
+            ratings_ahead = send(r_hbm.at[SUB - 1], rating_p, m_send.at[0], m_recv.at[0], others[0])
+        if mirrored and s == SUB - 2:
+            users_ahead = send(ulow.at[pl.ds(0, rows)], u_p, m_send.at[1], m_recv.at[1], others[0])
         wait_bytes(ss_in.at[s], s_recv.at[s])
         total = ss[s] + jnp.sum(ss_in[s], axis=0)
         mean = jnp.sum(total, axis=1, keepdims=True) / (nb * cols * rank)
@@ -235,6 +283,7 @@
     cols = ratings.shape[2]
     ct = cols // tile
     counts = -(-SUB * ct // 8) * 8
+    marks = -(-2 * (rows // tile) * ct // 8) * 8
     dma = pltpu.SemaphoreType.DMA
     vmem = pltpu.VMEM
     hbm = pl.BlockSpec(memory_space=pl.ANY)
@@ -251,8 +300,8 @@
             vmem((cols, rank), BF16),
             vmem((SUB, cols, rank), F32),
             vmem((cols, rank), F32),
-            vmem((rows, rank), BF16),
-            vmem((rows, cols), BF16),
+            vmem((2 * rows, rank), BF16),
+            vmem((2 * rows, cols), BF16),
             vmem((counts, rank), F32),
             vmem((nu - 1, counts, rank), F32),
             vmem((SUB, cols, rank), BF16),
@@ -272,6 +321,12 @@
             dma((SUB,)), dma((SUB,)),
             pltpu.SemaphoreType.REGULAR, pltpu.SemaphoreType.REGULAR,
             pltpu.SemaphoreType.REGULAR((len(SIDES),)),
+            vmem((rows, cols), BF16),
+            vmem((rows, cols), F32),
+            vmem((rows, rank), BF16),
+            vmem((marks, tile), F32),
+            vmem((marks, tile), F32),
+            dma((3,)), dma((3,)),
         ],
         compiler_params=pltpu.CompilerParams(collective_id=0, has_side_effects=True),
     )(user_factors, item_factors, ratings, jnp.swapaxes(tile_pattern, 1, 2), jnp.swapaxes(tile_scale, 1, 2))

time: 36.2 us -> 34.6 us (0.956)
  Pallas kernels: 35.4 us -> 33.8 us
    pallas_call x1, Pallas kernels: 34.7 us -> 33.1 us  [shards(): pl.pallas_call(functools.partial(kernel, nb, nu, tile), out_shape=(vmem(u...]
where the time goes in v3:
time: 34.6 us; the launch traced here: 34.4 us
  Pallas kernels  33.8 us (98%)
  between operations  0.64 us (2%)
    pallas_call x1, Pallas kernels, shards(): pl.pallas_call(functools.partial(kernel, nb, nu, tile), out_shape=(vmem(u...  33.1 us
    pallas_call x1, Pallas kernels, shards(): pl.pallas_call(hand_over, out_shape=(jax.ShapeDtypeStruct(user_factors.sh...  0.74 us

profile of v3, /device:TPU:0, one launch (start us, length us, event | category | flops | bytes accessed | tf_op | source)
XLA Modules:
  0.0 34.4 jit_solution(10193808734126808636)
XLA Ops:
  0.6 33.1 %shard_map.68 = (f32[512,128]{1,0:T(8,128)S(1)}, f32[128,128]{1,0:T(8,128)S(1)}) custom-call(f32[512,128]{1,0:T(8,128)} %u_hbm.1, f32[128,128]{1,0:T(8,128)} %v_hbm.1, bf16[3,512,256]{2,1,0:T(8,128)(2,1)} %r_hbm.1, s32[3,2,4]{2,1,0:T(2,128)} %bitcast.2, f32[3,2,4]{2,1,0:T(2,128)} %bitcast.3), custom_call_target="tpu_custom_call" | custom-call | tf_op jit(solution)/shard_map/pallas_call | solution.py:292
  33.7 0.7 %shard_map.69 = (f32[512,128]{1,0:T(8,128)}, f32[128,128]{1,0:T(8,128)}) custom-call(f32[512,128]{1,0:T(8,128)S(1)} %get-tuple-element.4.u, f32[128,128]{1,0:T(8,128)S(1)} %get-tuple-element.5.v), custom_call_target="tpu_custom_call" | custom-call | tf_op jit(solution)/shard_map/pallas_call | solution.py:333

commit v4 on v3

--- a/solution.py
+++ b/solution.py
@@ -175,19 +175,21 @@
             return jnp.concatenate(out, axis=1)
 
         sets = [(u, 0, own_tile)] + ([(u_p, rows, partner_tile)] if both else [])
-        for a in range(rt):
-            for held, start, tile_of in sets:
-                span = slice(a * tile, (a + 1) * tile)
-                place = slice(start + a * tile, start + (a + 1) * tile)
-                old = held[span, :].astype(F32)
-                one = errors(old.astype(BF16), a, tile_of)
-                grad = jnp.dot(one, v_low, preferred_element_type=F32) + penalty * old
-                new = old - user_step * grad
-                if held is u:
-                    u[span, :] = new
-                low = new.astype(BF16)
-                ulow[place, :] = low
-                err[place, :] = errors(low, a, tile_of)
+        work = [(held, start, tile_of, a) for a in range(rt) for held, start, tile_of in sets]
+        olds = [held[a * tile:(a + 1) * tile, :].astype(F32) for held, _, _, a in work]
+        ones = [errors(old.astype(BF16), a, tile_of) for old, (_, _, tile_of, a) in zip(olds, work)]
+        news = [
+            old - user_step * (jnp.dot(one, v_low, preferred_element_type=F32) + penalty * old)
+            for old, one in zip(olds, ones)
+        ]
+        lows = [new.astype(BF16) for new in news]
+        seconds = [errors(low, a, tile_of) for low, (_, _, tile_of, a) in zip(lows, work)]
+        for (held, start, _, a), new, low, second in zip(work, news, lows, seconds):
+            place = slice(start + a * tile, start + (a + 1) * tile)
+            ulow[place, :] = low
+            err[place, :] = second
+            if held is u:
+                u[place, :] = new
 
         exchanged = []
         for j in range(ct):

time: 34.6 us -> 33.3 us (0.962)
  Pallas kernels: 33.8 us -> 32.5 us
    pallas_call x1, Pallas kernels: 33.1 us -> 31.7 us  [shards(): pl.pallas_call(functools.partial(kernel, nb, nu, tile), out_shape=(vmem(u...]
where the time goes in v4:
time: 33.3 us; the launch traced here: 33.1 us
  Pallas kernels  32.5 us (98%)
  between operations  0.64 us (2%)
    pallas_call x1, Pallas kernels, shards(): pl.pallas_call(functools.partial(kernel, nb, nu, tile), out_shape=(vmem(u...  31.7 us
    pallas_call x1, Pallas kernels, shards(): pl.pallas_call(hand_over, out_shape=(jax.ShapeDtypeStruct(user_factors.sh...  0.74 us

profile of v4, /device:TPU:0, one launch (start us, length us, event | category | flops | bytes accessed | tf_op | source)
XLA Modules:
  0.0 33.1 jit_solution(824645819810497531)
XLA Ops:
  0.6 31.7 %shard_map.68 = (f32[512,128]{1,0:T(8,128)S(1)}, f32[128,128]{1,0:T(8,128)S(1)}) custom-call(f32[512,128]{1,0:T(8,128)} %u_hbm.1, f32[128,128]{1,0:T(8,128)} %v_hbm.1, bf16[3,512,256]{2,1,0:T(8,128)(2,1)} %r_hbm.1, s32[3,2,4]{2,1,0:T(2,128)} %bitcast.2, f32[3,2,4]{2,1,0:T(2,128)} %bitcast.3), custom_call_target="tpu_custom_call" | custom-call | tf_op jit(solution)/shard_map/pallas_call | solution.py:294
  32.4 0.7 %shard_map.69 = (f32[512,128]{1,0:T(8,128)}, f32[128,128]{1,0:T(8,128)}) custom-call(f32[512,128]{1,0:T(8,128)S(1)} %get-tuple-element.4.u, f32[128,128]{1,0:T(8,128)S(1)} %get-tuple-element.5.v), custom_call_target="tpu_custom_call" | custom-call | tf_op jit(solution)/shard_map/pallas_call | solution.py:335
